TPU v7x, 32 devices: a whole 2x2x4 slice. The times are simulated.
32 devices in a mesh: groups: 2 (over y), feat: 4 (over z), head: 4 (over x, core).
Axes of the slice: x: 2, y: 2, z: 4, core: 2. Of those that a mesh axis runs over, the one named last changes fastest.
Arguments:
- token_ids: int32 [32], P('groups'), parts along dimension 0, may hold values from 0 to 75967
- embedding: bfloat16 [75968, 5120], P('head', 'feat'), may hold values from -16 to 16
- retained: bfloat16 [2, 32, 8, 8256, 128], P(None, 'groups', 'head', 'feat'), parts along dimension 1, may hold values from -0.29882812 to 0.29882812
- query_weight: bfloat16 [2, 5120, 5120], P(None, 'feat', 'head'), may hold values from -0.078125 to 0.078125
- key_weight: bfloat16 [2, 5120, 1024], P(None, 'feat', 'head'), may hold values from -0.078125 to 0.078125
- value_weight: bfloat16 [2, 5120, 1024], P(None, 'feat', 'head'), may hold values from -0.078125 to 0.078125
- gate_weight: bfloat16 [2, 5120, 8], P(None, 'feat', 'head'), may hold values from -0.078125 to 0.078125
- gate_bias: float32 [2, 8], P(None, 'head'), may hold values from -4 to 3
- norm_gain: float32 [2, 5120], P(None, 'feat'), may hold values from 0.1 to 1.9
- read_gain: float32 [2, 128], replicated, may hold values from 0.1 to 1.9
- out_weight: bfloat16 [2, 5120, 5120], P(None, 'head', 'feat'), may hold values from -0.078125 to 0.078125
Outputs:
- hidden_out: bfloat16 [32, 5120], P('groups', 'feat'), parts along dimension 0
There are 2 independent parts, one for each index of `groups`. A program takes and returns all parts, laid end to end along the dimension named above; an argument that names none is the same for every part. Nothing has to cross between parts.
All inputs are finite; a program needn't handle non-finite values.
Results may differ from a plain program's by a relative error of at most 0.01345.
The roundings to bfloat16 on the way count: a program that leaves them out, or rounds other values in their place, can miss the bound.
Values may be sent and summed in bfloat16 or wider, within the bound.
A program may use at most 192 MiB of HBM per device.

v0:
```python
import functools
import math

import jax
import jax.numpy as jnp
from jax import lax
from jax.experimental import pallas as pl
from jax.experimental.pallas import tpu as pltpu
from jax.sharding import PartitionSpec as P

MESH = pl.DeviceIdType.MESH
F32 = jnp.float32
BF16 = jnp.bfloat16
SEND = jnp.bfloat16


def lookup(ids_ref, table_hbm, picked_ref, rows_buf, row_sem):
    requests, width = picked_ref.shape
    table_rows = table_hbm.shape[0]
    base = lax.axis_index("head") * table_rows
    window = rows_buf.shape[0] // requests
    out_row = lax.broadcasted_iota(jnp.int32, (requests, requests * window), 0)
    column = lax.broadcasted_iota(jnp.int32, (requests, requests * window), 1)
    select = jnp.zeros((requests, requests * window), F32)
    copies = []
    for i in range(requests):
        local = ids_ref[i] - base
        row = jnp.clip(local, 0, table_rows - 1)
        first = pl.multiple_of(jnp.minimum((row // 8) * 8, table_rows - window), 8)
        copy = pltpu.make_async_copy(
            table_hbm.at[pl.ds(first, window)],
            rows_buf.at[pl.ds(i * window, window)],
            row_sem.at[i],
        )
        copy.start()
        copies.append(copy)
        value = jnp.where(local == row, 1.0, 0.0)
        hit = (out_row == i) & (column == i * window + row - first)
        select = jnp.where(hit, value, select)
    for copy in copies:
        copy.wait()
    picked_ref[...] = jnp.dot(
        select.astype(BF16), rows_buf[...], preferred_element_type=F32
    ).astype(BF16)


def partner_of(me, count, turn):
    if count == 4:
        return (3 - me, lax.rem(me + 2, 4), me + 1 - 2 * lax.rem(me, 2))[turn - 1]
    return lax.rem(me + turn, count)


def kernel(
    feat_count,
    head_count,
    picked_ref,
    retained_hbm,
    query_hbm,
    key_hbm,
    value_hbm,
    gate_hbm,
    bias_ref,
    gain_ref,
    read_ref,
    out_hbm,
    result_ref,
    state,
    query_w,
    key_w,
    value_w,
    gate_w,
    out_w,
    pick_buf,
    query_buf,
    pair_buf,
    small_buf,
    read_buf,
    branch_buf,
    left_sel,
    right_sel,
    pair_scale,
    phi,
    history,
    partial,
    load_sem,
    state_sem,
    send_sem,
    recv_sem,
):
    layers, requests, heads, block, head_size = state.shape
    width = query_w.shape[1]
    query_columns = query_w.shape[2]
    kv_columns = key_w.shape[2]
    chunks, chunk = branch_buf.shape[1], branch_buf.shape[4]
    group = query_columns // (heads * head_size)
    me_feat = lax.axis_index("feat")
    me_head = lax.axis_index("head")

    loads = []
    for layer in range(layers):
        pairs = [(gate_hbm, gate_w), (query_hbm, query_w), (key_hbm, key_w), (value_hbm, value_w)]
        for slot, (source, target) in enumerate(pairs):
            copy = pltpu.make_async_copy(
                source.at[layer], target.at[layer], load_sem.at[layer, slot]
            )
            copy.start()
            loads.append((layer, slot, copy))
        for r in range(requests):
            pltpu.make_async_copy(
                retained_hbm.at[layer, r], state.at[layer, r], state_sem.at[layer, r]
            ).start()
        copy = pltpu.make_async_copy(out_hbm.at[layer], out_w.at[layer], load_sem.at[layer, 4])
        copy.start()
        loads.append((layer, 4, copy))
    load = {(layer, slot): copy for layer, slot, copy in loads}

    barrier = pltpu.get_barrier_semaphore()
    for axis, count, me in (("feat", feat_count, me_feat), ("head", head_count, me_head)):
        for d in range(1, count):
            pl.semaphore_signal(
                barrier, inc=1, device_id={axis: lax.rem(me + d, count)}, device_id_type=MESH
            )
    pl.semaphore_wait(barrier, feat_count + head_count - 2)

    used = [0]

    def exchange(axis, count, me, source_of, target):
        copies = []
        for d in range(1, count):
            copy = pltpu.make_async_remote_copy(
                src_ref=source_of,
                dst_ref=target,
                send_sem=send_sem.at[used[0]],
                recv_sem=recv_sem.at[used[0]],
                device_id={axis: partner_of(me, count, d)},
                device_id_type=MESH,
            )
            copy.start()
            copies.append(copy)
            used[0] += 1
        return copies

    pending = exchange("head", head_count, me_head, picked_ref, pick_buf.at[me_head])
    pick_buf[me_head] = picked_ref[...]

    feature = lax.broadcasted_iota(jnp.int32, (head_size, block), 1) + me_feat * block
    position = lax.broadcasted_iota(jnp.int32, (head_size, block), 0)
    begin = position * head_size - (position * (position - 1)) // 2
    inside = (feature >= begin) & (feature < begin + head_size - position)
    left_sel[...] = jnp.where(inside, 1.0, 0.0).astype(BF16)
    partner = jnp.sum(jnp.where(inside, feature - begin + position, 0), axis=0, keepdims=True)
    right_sel[...] = jnp.where(position == partner, 1.0, 0.0).astype(BF16)
    first = jnp.sum(jnp.where(inside, position, 0), axis=0, keepdims=True)
    pair_scale[...] = jnp.where(first == partner, 1.0, math.sqrt(2.0)).astype(F32)

    slots = requests * 8
    compact = requests * group
    span = group * head_size
    unroll = 4 if requests % 4 == 0 else 1

    def place(rows, columns, swap):
        a = lax.broadcasted_iota(jnp.int32, (rows, columns), 0)
        b = lax.broadcasted_iota(jnp.int32, (rows, columns), 1)
        wide, packed = (b, a) if swap else (a, b)
        match = (packed == (wide % 8) * requests + wide // 8) & (wide % 8 < group)
        return jnp.where(match, 1.0, 0.0).astype(BF16)

    spread = place(slots, compact, False)
    gather = place(compact, slots, True)

    for copy in pending:
        copy.wait()
    stream = pick_buf[0].astype(F32)
    for i in range(1, head_count):
        stream = stream + pick_buf[i].astype(F32)

    for layer in range(layers):
        gained = (stream * gain_ref[layer : layer + 1, :]).astype(BF16)
        square = jnp.sum(stream * stream, axis=1, keepdims=True)
        load[layer, 0].wait()
        gained_wide = gained.astype(F32)
        gates = gate_w[layer].astype(F32)
        lane = lax.broadcasted_iota(jnp.int32, (requests, 128), 1)
        small = jnp.where(lane == heads, square, 0.0)
        for h in range(heads):
            along = jnp.sum(gained_wide * gates[h : h + 1, :], axis=1, keepdims=True)
            small = jnp.where(lane == h, along, small)
        small_buf[layer, me_feat] = small
        small_copies = exchange(
            "feat", feat_count, me_feat, small_buf.at[layer, me_feat], small_buf.at[layer, me_feat]
        )
        load[layer, 1].wait()
        query_copies = []
        for h in range(heads):
            query_buf[layer, h, me_feat] = jnp.dot(
                gained, query_w[layer, :, h * span : (h + 1) * span], preferred_element_type=F32
            ).astype(SEND)
            own = query_buf.at[layer, h, me_feat]
            query_copies.append(exchange("feat", feat_count, me_feat, own, own))
        for slot, weight in ((2, key_w), (3, value_w)):
            load[layer, slot].wait()
            pair_buf[layer, me_feat, :, (slot - 2) * kv_columns : (slot - 1) * kv_columns] = jnp.dot(
                gained, weight[layer], preferred_element_type=F32
            ).astype(SEND)
        own = pair_buf.at[layer, me_feat]
        pair_copies = exchange("feat", feat_count, me_feat, own, own)
        for copy in small_copies:
            copy.wait()
        totals = small_buf[layer, 0]
        for i in range(1, feat_count):
            totals = totals + small_buf[layer, i]
        inverse = lax.rsqrt(totals[:, heads : heads + 1] / (width * feat_count) + 1e-06)
        gate = totals[:, :heads] * inverse + bias_ref[layer : layer + 1, :]
        decay = 1.0 / (1.0 + jnp.exp(gate))
        query = []
        read_copies = []
        for h in range(heads):
            for copy in query_copies[h]:
                copy.wait()
            summed = query_buf[layer, h, 0].astype(F32)
            for i in range(1, feat_count):
                summed = summed + query_buf[layer, h, i].astype(F32)
            summed = (summed * inverse).astype(BF16)
            rows = [summed[:, i * head_size : (i + 1) * head_size] for i in range(group)]
            query.append(rows)
            stacked = jnp.concatenate(rows, axis=0)
            placed = jnp.dot(spread, stacked, preferred_element_type=F32).astype(BF16)
            for start in range(0, block, 256):
                stop = min(start + 256, block)
                left = jnp.dot(placed, left_sel[:, start:stop], preferred_element_type=F32)
                right = jnp.dot(placed, right_sel[:, start:stop], preferred_element_type=F32)
                phi[:, start:stop] = left * right * pair_scale[:, start:stop]

            def read(step, carry, h=h):
                for extra in range(unroll):
                    r = step * unroll + extra
                    if h == 0:
                        pltpu.make_async_copy(
                            retained_hbm.at[layer, r], state.at[layer, r], state_sem.at[layer, r]
                        ).wait()
                for extra in range(unroll):
                    r = step * unroll + extra
                    at = pl.ds(pl.multiple_of(r * 8, 8), 8)
                    history[at, :] = jnp.dot(
                        phi[at, :].astype(BF16), state[layer, r, h], preferred_element_type=F32
                    )
                return carry

            lax.fori_loop(0, requests // unroll, read, 0)
            packed = jnp.dot(gather, history[...].astype(BF16), preferred_element_type=F32)
            read_buf[layer, h, me_feat] = packed.astype(SEND)
            own = read_buf.at[layer, h, me_feat]
            read_copies.append(exchange("feat", feat_count, me_feat, own, own))
        for copy in pair_copies:
            copy.wait()
        summed = pair_buf[layer, 0].astype(F32)
        for i in range(1, feat_count):
            summed = summed + pair_buf[layer, i].astype(F32)
        summed = (summed * inverse).astype(BF16).astype(F32)
        branch_copies = []
        load[layer, 4].wait()
        for h in range(heads):
            key = summed[:, h * head_size : (h + 1) * head_size]
            value = summed[:, kv_columns + h * head_size : kv_columns + (h + 1) * head_size]
            cross = []
            for i in range(group):
                along = jnp.sum(query[h][i].astype(F32) * key, axis=1, keepdims=True)
                cross.append(along * along / head_size)
            for copy in read_copies[h]:
                copy.wait()
            reads = read_buf[layer, h, 0].astype(F32)
            for i in range(1, feat_count):
                reads = reads + read_buf[layer, h, i].astype(F32)
            mixed = []
            for i in range(group):
                readout = (
                    decay[:, h : h + 1] * reads[i * requests : (i + 1) * requests]
                    + cross[i] * value
                )
                scale = lax.rsqrt(jnp.mean(readout * readout, axis=1, keepdims=True) + 1e-06)
                mixed.append((readout * scale * read_ref[layer : layer + 1, :]).astype(BF16))
            mixed = jnp.concatenate(mixed, axis=1)
            for c in range(chunks):
                columns = slice(c * chunk, (c + 1) * chunk)
                part = jnp.dot(
                    mixed,
                    out_w[layer, h * span : (h + 1) * span, columns],
                    preferred_element_type=F32,
                )
                if h > 0:
                    part = part + partial[:, columns]
                if h < heads - 1:
                    partial[:, columns] = part
                else:
                    branch_buf[layer, c, me_head] = part.astype(SEND)
                    own = branch_buf.at[layer, c, me_head]
                    branch_copies.append(exchange("head", head_count, me_head, own, own))
        branch = []
        for c in range(chunks):
            for copy in branch_copies[c]:
                copy.wait()
            total = branch_buf[layer, c, 0].astype(F32)
            for i in range(1, head_count):
                total = total + branch_buf[layer, c, i].astype(F32)
            branch.append(total)
        branch = jnp.concatenate(branch, axis=1) if chunks > 1 else branch[0]
        stream_out = (stream + branch).astype(BF16)
        stream = stream_out.astype(F32)
    result_ref[...] = stream_out


def body(
    feat_count,
    head_count,
    token_ids,
    embedding,
    retained,
    query_weight,
    key_weight,
    value_weight,
    gate_weight,
    gate_bias,
    norm_gain,
    read_gain,
    out_weight,
):
    layers, requests, heads, block, head_size = retained.shape
    width = query_weight.shape[1]
    query_columns = query_weight.shape[2]
    kv_columns = key_weight.shape[2]
    group = query_columns // (heads * head_size)
    chunks = 2 if width % 256 == 0 else 1
    copies = (head_count - 1) + layers * (
        (2 + 2 * heads) * (feat_count - 1) + chunks * (head_count - 1)
    )
    gate_rows = jnp.swapaxes(gate_weight, 1, 2)
    window = 16
    picked = pl.pallas_call(
        lookup,
        out_shape=jax.ShapeDtypeStruct((requests, width), BF16),
        in_specs=[pl.BlockSpec(memory_space=pltpu.SMEM), pl.BlockSpec(memory_space=pl.ANY)],
        out_specs=pl.BlockSpec(memory_space=pltpu.VMEM),
        scratch_shapes=[
            pltpu.VMEM((requests * window, width), BF16),
            pltpu.SemaphoreType.DMA((requests,)),
        ],
    )(token_ids, embedding)
    anywhere = pl.BlockSpec(memory_space=pl.ANY)
    local = pl.BlockSpec(memory_space=pltpu.VMEM)
    return pl.pallas_call(
        functools.partial(kernel, feat_count, head_count),
        out_shape=jax.ShapeDtypeStruct((requests, width), BF16),
        in_specs=[local] + [anywhere] * 5 + [local] * 3 + [anywhere],
        out_specs=local,
        scratch_shapes=[
            pltpu.VMEM(retained.shape, BF16),
            pltpu.VMEM(query_weight.shape, BF16),
            pltpu.VMEM(key_weight.shape, BF16),
            pltpu.VMEM(value_weight.shape, BF16),
            pltpu.VMEM(gate_rows.shape, BF16),
            pltpu.VMEM(out_weight.shape, BF16),
            pltpu.VMEM((head_count, requests, width), BF16),
            pltpu.VMEM((layers, heads, feat_count, requests, group * head_size), SEND),
            pltpu.VMEM((layers, feat_count, requests, 2 * kv_columns), SEND),
            pltpu.VMEM((layers, feat_count, requests, 128), F32),
            pltpu.VMEM((layers, heads, feat_count, requests * group, head_size), SEND),
            pltpu.VMEM((layers, chunks, head_count, requests, width // chunks), SEND),
            pltpu.VMEM((head_size, block), BF16),
            pltpu.VMEM((head_size, block), BF16),
            pltpu.VMEM((1, block), F32),
            pltpu.VMEM((requests * 8, block), F32),
            pltpu.VMEM((requests * 8, head_size), F32),
            pltpu.VMEM((requests, width), F32),
            pltpu.SemaphoreType.DMA((layers, 5)),
            pltpu.SemaphoreType.DMA((layers, requests)),
            pltpu.SemaphoreType.DMA((copies,)),
            pltpu.SemaphoreType.DMA((copies,)),
        ],
        compiler_params=pltpu.CompilerParams(
            collective_id=0, has_side_effects=True, vmem_limit_bytes=66_000_000
        ),
    )(
        picked,
        retained,
        query_weight,
        key_weight,
        value_weight,
        gate_rows,
        gate_bias,
        norm_gain,
        read_gain,
        out_weight,
    )


def solution(mesh):
    return jax.shard_map(
        functools.partial(body, mesh.shape["feat"], mesh.shape["head"]),
        mesh=mesh,
        in_specs=(
            P("groups"),
            P("head", "feat"),
            P(None, "groups", "head", "feat", None),
            P(None, "feat", "head"),
            P(None, "feat", "head"),
            P(None, "feat", "head"),
            P(None, "feat", "head"),
            P(None, "head"),
            P(None, "feat"),
            P(),
            P(None, "head", "feat"),
        ),
        out_specs=P("groups", "feat"),
        check_vma=False,
    )
```

profile of v0, /device:TPU:0, one launch (start us, length us, event | category | flops | bytes accessed | tf_op | source)
XLA Modules:
  0.0 55.0 jit_solution(12871542085666448263)
XLA Ops:
  0.0 3.1 %shard_map.109.picked_ref = bf16[16,1280]{1,0:T(8,128)(2,1)} custom-call(s32[16]{0:T(128)} %ids_ref.1, bf16[18992,1280]{1,0:T(8,128)(2,1)} %table_hbm.1), custom_call_target="tpu_custom_call" | custom-call | tf_op jit(solution)/shard_map/pallas_call | solution.py:338
  3.1 50.5 %shard_map.110 = bf16[16,1280]{1,0:T(8,128)(2,1)} custom-call(bf16[16,1280]{1,0:T(8,128)(2,1)} %shard_map.109.picked_ref, bf16[2,16,2,2064,128]{4,3,2,1,0:T(8,128)(2,1)} %retained_hbm.1, bf16[2,1280,1280]{2,1,0:T(8,128)(2,1)} %query_hbm.1, bf16[2,1280,256]{2,1,0:T(8,128)(2,1)} %key_hbm.1, bf16[2,1280,256]{2,1,0:T(8,128)(2,1)} %value_hbm.1, ...), custom_call_target="tpu_custom_call" | custom-call | tf_op jit(solution)/shard_map/pallas_call | solution.py:350
  53.6 1.4 %copy.13 = bf16[16,1280]{1,0:T(8,128)(2,1)} copy(bf16[16,1280]{1,0:T(8,128)(2,1)} %shard_map.110) | data formatting | bytes 81920
where the time goes:
time: 55.4 us; the launch traced here: 55 us
  Pallas kernels  53.6 us (97%)
  local copies, waits for them, and re-layouts  1.4 us (3%)
    pallas_call x1, Pallas kernels, body(): pl.pallas_call(functools.partial(kernel, feat_count, head_count), out_sha...  50.5 us
    pallas_call x1, Pallas kernels, body(): pl.pallas_call(lookup, out_shape=jax.ShapeDtypeStruct((requests, width),...  3.1 us
    unnamed x1, local copies, waits for them, and re-layouts  1.4 us

commit v1 on v0

--- a/solution.py
+++ b/solution.py
@@ -96,23 +96,27 @@
     me_feat = lax.axis_index("feat")
     me_head = lax.axis_index("head")
 
-    loads = []
-    for layer in range(layers):
+    load = {}
+
+    def load_inputs(layer):
         pairs = [(gate_hbm, gate_w), (query_hbm, query_w), (key_hbm, key_w), (value_hbm, value_w)]
         for slot, (source, target) in enumerate(pairs):
-            copy = pltpu.make_async_copy(
+            load[layer, slot] = pltpu.make_async_copy(
                 source.at[layer], target.at[layer], load_sem.at[layer, slot]
             )
-            copy.start()
-            loads.append((layer, slot, copy))
+            load[layer, slot].start()
+
+    def load_state(layer):
         for r in range(requests):
             pltpu.make_async_copy(
                 retained_hbm.at[layer, r], state.at[layer, r], state_sem.at[layer, r]
             ).start()
-        copy = pltpu.make_async_copy(out_hbm.at[layer], out_w.at[layer], load_sem.at[layer, 4])
-        copy.start()
-        loads.append((layer, 4, copy))
-    load = {(layer, slot): copy for layer, slot, copy in loads}
+        load[layer, 4] = pltpu.make_async_copy(
+            out_hbm.at[layer], out_w.at[layer], load_sem.at[layer, 4]
+        )
+        load[layer, 4].start()
+
+    load_inputs(0)
 
     barrier = pltpu.get_barrier_semaphore()
     for axis, count, me in (("feat", feat_count, me_feat), ("head", head_count, me_head)):
@@ -141,6 +145,7 @@
         return copies
 
     pending = exchange("head", head_count, me_head, picked_ref, pick_buf.at[me_head])
+    load_state(0)
     pick_buf[me_head] = picked_ref[...]
 
     feature = lax.broadcasted_iota(jnp.int32, (head_size, block), 1) + me_feat * block
@@ -204,6 +209,9 @@
             ).astype(SEND)
         own = pair_buf.at[layer, me_feat]
         pair_copies = exchange("feat", feat_count, me_feat, own, own)
+        if layer + 1 < layers:
+            load_inputs(layer + 1)
+            load_state(layer + 1)
         for copy in small_copies:
             copy.wait()
         totals = small_buf[layer, 0]

time: 55.4 us -> 54 us (0.975)
  Pallas kernels: 53.6 us -> 52.3 us
    pallas_call x1, Pallas kernels: 50.5 us -> 49 us  [body(): pl.pallas_call(functools.partial(kernel, feat_count, head_count), out_sha...]
where the time goes in v1:
time: 54 us; the launch traced here: 53.7 us
  Pallas kernels  52.3 us (97%)
  local copies, waits for them, and re-layouts  1.4 us (3%)
    pallas_call x1, Pallas kernels, body(): pl.pallas_call(functools.partial(kernel, feat_count, head_count), out_sha...  49 us
    pallas_call x1, Pallas kernels, body(): pl.pallas_call(lookup, out_shape=jax.ShapeDtypeStruct((requests, width),...  3.36 us
    unnamed x1, local copies, waits for them, and re-layouts  1.4 us

profile of v1, /device:TPU:0, one launch (start us, length us, event | category | flops | bytes accessed | tf_op | source)
XLA Modules:
  0.0 53.7 jit_solution(13778521845664550036)
XLA Ops:
  0.0 3.4 %shard_map.109.picked_ref = bf16[16,1280]{1,0:T(8,128)(2,1)} custom-call(s32[16]{0:T(128)} %ids_ref.1, bf16[18992,1280]{1,0:T(8,128)(2,1)} %table_hbm.1), custom_call_target="tpu_custom_call" | custom-call | tf_op jit(solution)/shard_map/pallas_call | solution.py:346
  3.4 49.0 %shard_map.110 = bf16[16,1280]{1,0:T(8,128)(2,1)} custom-call(bf16[16,1280]{1,0:T(8,128)(2,1)} %shard_map.109.picked_ref, bf16[2,16,2,2064,128]{4,3,2,1,0:T(8,128)(2,1)} %retained_hbm.1, bf16[2,1280,1280]{2,1,0:T(8,128)(2,1)} %query_hbm.1, bf16[2,1280,256]{2,1,0:T(8,128)(2,1)} %key_hbm.1, bf16[2,1280,256]{2,1,0:T(8,128)(2,1)} %value_hbm.1, ...), custom_call_target="tpu_custom_call" | custom-call | tf_op jit(solution)/shard_map/pallas_call | solution.py:358
  52.3 1.4 %copy.13 = bf16[16,1280]{1,0:T(8,128)(2,1)} copy(bf16[16,1280]{1,0:T(8,128)(2,1)} %shard_map.110) | data formatting | bytes 81920
